TPU v7x, 32 devices: a whole 2x2x4 slice. The times are simulated.
32 devices in a mesh: ens: 2 (over y), space: 16 (over z, x, core).
Axes of the slice: x: 2, y: 2, z: 4, core: 2. Of those that a mesh axis runs over, the one named last changes fastest.
Arguments:
- node_states: bfloat16 [2, 2048, 1024], P('ens', 'space'), may hold values from -6 to 6
- query: bfloat16 [2, 2048, 512], P('ens', 'space'), may hold values from -240 to 240
- key: bfloat16 [2, 2048, 512], P('ens', 'space'), may hold values from -6 to 6
- value: bfloat16 [2, 2048, 512], P('ens', 'space'), may hold values from -6 to 6
- out_weight: bfloat16 [512, 1024], replicated, may hold values from -0.25 to 0.25
- dec_weight: bfloat16 [100, 1024], replicated, may hold values from -0.1875 to 0.1875
- target: float32 [100, 16384], P(None, 'space'), may hold values from -6 to 6
- area_weight: float32 [16384], P('space'), may hold values from 0.25 to 2.5
- var_weight: float32 [100], replicated, may hold values from 0.5 to 5
- edges: int32 [3, 16384], P(None, 'space'), may hold values from 0 to 2047, as said below
- edge_weight: float32 [3, 16384], P(None, 'space'), may hold values from 0.1 to 0.6
- windows: int32 [2, 16], P(None, 'space'), may hold values from 0 to 2048, as said below
Outputs:
- grad_states: bfloat16 [2, 2048, 1024], P('ens', 'space')
- grad_query: bfloat16 [2, 2048, 512], P('ens', 'space')
- grad_key: bfloat16 [2, 2048, 512], P('ens', 'space')
- grad_value: bfloat16 [2, 2048, 512], P('ens', 'space')
- grad_wo: float32 [512, 1024], P('space')
- grad_dec: float32 [100, 1024], replicated
Inputs may be any that keep to these rules, and one draw needn't show every extreme that they name: The edges of a point among the 1024 points p with p // 1024 = d name nodes from d * 128 - 128 to d * 128 + 2 * 128 - 1; both ends are named in every draw. For the block b of nodes s = b * 128 to s + 127: max(0, s - 128) <= windows[0, b] <= s and s + 128 <= windows[1, b] <= min(2048, s + 256); the outer ends s - 128 and s + 256 are reached by some block in every draw.
All inputs are finite; a program needn't handle non-finite values.
Results may differ from a plain program's by a relative error of at most 0.017.
Values may be sent and summed in bfloat16 or wider, within the bound.
A program may use at most 64 MiB of HBM per device.

v0:
```python
import functools
import math

import jax
import jax.numpy as jnp
from jax import lax
from jax.experimental import pallas as pl
from jax.experimental.pallas import tpu as pltpu
from jax.sharding import PartitionSpec as P

HEAD_DIM = 64
BLOCK = 128
INNER = 4
LANES = 128
SMOOTH_SQUARE = 0.0625
MASKED_SCORE = -1e30
F32 = jnp.float32
BF16 = jnp.bfloat16
NT = (((1,), (1,)), ((), ()))
TN = (((0,), (0,)), ((), ()))


def smooth_slope(diff_value):
    return diff_value * lax.rsqrt(diff_value * diff_value + SMOOTH_SQUARE)


def dot(a, b, dims=(((1,), (0,)), ((), ()))):
    return lax.dot_general(a, b, dims, preferred_element_type=F32)


def kernel(
    n_e,
    n_s,
    states_hbm,
    q_hbm,
    k_hbm,
    v_hbm,
    ow_hbm,
    dec_hbm,
    target_hbm,
    area_hbm,
    var_hbm,
    edges_hbm,
    ew_hbm,
    win_hbm,
    gs_ref,
    gq_ref,
    gk_ref,
    gv_ref,
    gwo_ref,
    gdec_ref,
    states_ref,
    q_ref,
    k_ref,
    v_ref,
    ow_ref,
    dec_ref,
    target_ref,
    area_ref,
    var_ref,
    edges_ref,
    ew_ref,
    win_ref,
    decp,
    wt,
    kh,
    tsend,
    text,
    gp,
    qsend,
    qrecv,
    prob,
    ao,
    go,
    kmid,
    vmid,
    bsend,
    brecv,
    csend,
    crecv,
    dsend,
    drecv,
    zsend,
    zrecv,
    fsend,
    frecv,
    agsend,
    dall,
    kv_s,
    kv_r,
    t_s,
    t_r,
    q_s,
    q_r,
    b_s,
    b_r,
    c_s,
    c_r,
    d_s,
    d_r,
    a_s,
    a_r,
    z_s,
    z_r,
    f_s,
    f_r,
    load_sem,
):
    e = lax.axis_index("ens")
    s = lax.axis_index("space")
    inner = math.gcd(n_s, INNER)
    outer = n_s // inner
    group = n_e * inner
    ring, seat = lax.div(s, inner), lax.rem(s, inner)
    n_dev = n_e * n_s
    me = e * n_s + s
    mine = e * inner + seat
    nodes, width = states_ref.shape
    att = q_ref.shape[1]
    pairs = att // LANES
    n_var = dec_ref.shape[0]
    var_pad = decp.shape[0]
    points = target_ref.shape[1]
    scale = 1.0 / math.sqrt(HEAD_DIM)
    has_left = s > 0
    has_right = s < n_s - 1
    sides = ((0, -1, has_left), (1, 1, has_right))

    def remote(src, dst, send_sem, recv_sem, ens, space):
        return pltpu.make_async_remote_copy(
            src_ref=src,
            dst_ref=dst,
            send_sem=send_sem,
            recv_sem=recv_sem,
            device_id=(ens, space),
            device_id_type=pl.DeviceIdType.MESH,
        )

    loads = {}
    for i, (name, source, held) in enumerate(
        (
            ("states", states_hbm, states_ref),
            ("dec", dec_hbm, dec_ref),
            ("k", k_hbm, k_ref),
            ("v", v_hbm, v_ref),
            ("edges", edges_hbm, edges_ref),
            ("ew", ew_hbm, ew_ref),
            ("target", target_hbm, target_ref),
            ("area", area_hbm, area_ref),
            ("var", var_hbm, var_ref),
            ("win", win_hbm, win_ref),
            ("q", q_hbm, q_ref),
            ("ow", ow_hbm, ow_ref),
        )
    ):
        loads[name] = pltpu.make_async_copy(source, held, load_sem.at[i])

    def loaded(*wanted):
        for name in wanted:
            loads[name].wait()

    barrier = pltpu.get_barrier_semaphore()

    def greet(ens, space):
        pl.semaphore_signal(
            barrier,
            inc=1,
            device_id=(ens, space),
            device_id_type=pl.DeviceIdType.MESH,
        )

    def plane_place(i):
        to = lax.rem(mine + i, group)
        return to, lax.div(to, inner), ring * inner + lax.rem(to, inner)

    def outer_place(i):
        to = lax.rem(ring + i, outer)
        return to, e, to * inner + seat

    @pl.loop(1, n_dev)
    def _(i):
        to = lax.rem(me + i, n_dev)
        greet(lax.div(to, n_s), lax.rem(to, n_s))

    for load in loads.values():
        load.start()

    for slot, _, present in sides:

        @pl.when(jnp.logical_not(present))
        def _():
            kh[slot] = jnp.zeros(kh.shape[1:], BF16)
            for j in range(n_e):
                text[j, 2 * slot] = jnp.zeros(text.shape[2:], BF16)
            qrecv[slot] = jnp.zeros(qrecv.shape[1:], BF16)
            brecv[slot] = jnp.zeros(brecv.shape[1:], BF16)

    decp[...] = jnp.zeros(decp.shape, BF16)
    loaded("states", "dec")
    decp[0:n_var, :] = dec_ref[...]
    own_t = dot(decp[...], states_ref[...], NT).astype(BF16)
    tsend[...] = own_t
    text[e, 1] = own_t

    loaded("edges", "ew")
    first = (s - 1) * nodes
    chunk = nodes
    for part in range(3):
        node_ids = first + part * chunk + lax.broadcasted_iota(jnp.int32, (chunk, points), 0)
        total = jnp.zeros((chunk, points), F32)
        for slot in range(edges_ref.shape[0]):
            total = total + jnp.where(
                node_ids == edges_ref[slot : slot + 1, :], ew_ref[slot : slot + 1, :], 0.0
            )
        wt[part * chunk : (part + 1) * chunk, :] = total.astype(BF16)

    loaded("k", "v")
    pl.semaphore_wait(barrier, n_dev - 1)

    def t_copies():
        for r in range(n_e):
            ens = lax.rem(e + r, n_e)
            for shift, present in ((0, None), (-1, has_left), (1, has_right)):
                if r == 0 and shift == 0:
                    continue
                spot = 1 - shift
                yield (
                    remote(
                        tsend,
                        text.at[e, spot],
                        t_s.at[r, shift + 1],
                        t_r.at[e, spot],
                        ens,
                        s + shift,
                    ),
                    remote(
                        tsend,
                        text.at[ens, shift + 1],
                        t_s.at[r, shift + 1],
                        t_r.at[ens, shift + 1],
                        ens,
                        s + shift,
                    ),
                    present,
                )

    def under(present, action):
        if present is None:
            action()
        else:
            pl.when(present)(action)

    for out, _, present in t_copies():
        under(present, out.start)

    def kv_copies(slot, shift, item):
        src = k_ref if item == 0 else v_ref
        out = remote(
            src,
            kh.at[1 - slot, item],
            kv_s.at[slot, item],
            kv_r.at[1 - slot, item],
            e,
            s + shift,
        )
        back = remote(
            src, kh.at[slot, item], kv_s.at[slot, item], kv_r.at[slot, item], e, s + shift
        )
        return out, back

    for slot, shift, present in sides:
        for item in range(2):
            under(present, kv_copies(slot, shift, item)[0].start)

    for _, back, present in t_copies():
        under(present, back.wait_recv)

    loaded("target", "area", "var", "win", "q", "ow")

    def predictions(member):
        cat = jnp.concatenate([text[member, i] for i in range(3)], axis=1)
        return dot(cat, wt[...])[0:n_var].astype(BF16).astype(F32)

    own_pred = predictions(e)
    slopes = smooth_slope(own_pred - target_ref[...])
    pair_sum = jnp.zeros_like(own_pred)
    for r in range(1, n_e):
        pair_sum = pair_sum + smooth_slope(own_pred - predictions(lax.rem(e + r, n_e)))
    slopes = slopes - pair_sum / (n_e - 1)
    square = (n_var, n_var)
    diagonal = lax.broadcasted_iota(jnp.int32, square, 0) == lax.broadcasted_iota(
        jnp.int32, square, 1
    )
    var_column = jnp.sum(jnp.where(diagonal, var_ref[...], 0.0), axis=1, keepdims=True)
    gp[...] = jnp.zeros(gp.shape, BF16)
    gp[0:n_var, :] = (area_ref[...] * var_column * slopes).astype(BF16)
    q_ext = dot(gp[...], wt[...], NT)
    qsend[0] = q_ext[:, 0:nodes].astype(BF16)
    qsend[1] = q_ext[:, 2 * nodes :].astype(BF16)

    def q_copies(slot, shift):
        out = remote(
            qsend.at[slot], qrecv.at[1 - slot], q_s.at[slot], q_r.at[1 - slot], e, s + shift
        )
        back = remote(
            qsend.at[slot], qrecv.at[slot], q_s.at[slot], q_r.at[slot], e, s + shift
        )
        return out, back

    for slot, shift, present in sides:
        under(present, q_copies(slot, shift)[0].start)

    blocks = win_ref.shape[0]
    key_place = first + lax.broadcasted_iota(jnp.int32, (1, 3 * nodes), 1)
    inside_rows = [
        (key_place >= win_ref[b : b + 1, 0:1]) & (key_place < win_ref[b : b + 1, 1:2])
        for b in range(blocks)
    ]
    heads_per = LANES // HEAD_DIM
    lane_head = lax.broadcasted_iota(jnp.int32, (nodes, LANES), 1) // HEAD_DIM

    def split_heads(x):
        x = x.astype(F32)
        return jnp.concatenate(
            [jnp.where(lane_head == h, x, 0.0).astype(BF16) for h in range(heads_per)], axis=0
        )

    def merge_heads(x):
        out = x[0:nodes]
        for h in range(1, heads_per):
            out = jnp.where(lane_head == h, x[h * nodes : (h + 1) * nodes], out)
        return out

    def extended(item, own_ref, columns):
        return jnp.concatenate(
            [kh[0, item, :, columns], own_ref[:, columns], kh[1, item, :, columns]], axis=0
        )

    def columns_of(p):
        return pl.ds(pl.multiple_of(p * LANES, LANES), LANES)

    def scaled_queries(columns):
        return split_heads(q_ref[:, columns].astype(F32) * scale)

    for slot, shift, present in sides:
        under(present, q_copies(slot, shift)[1].wait_recv)
    q_own = q_ext[:, nodes : 2 * nodes] + qrecv[0].astype(F32) + qrecv[1].astype(F32)
    q_rows = q_own.T.astype(BF16)
    dec_term = dot(q_own.astype(BF16), states_ref[...])
    var_rows, lanes = dsend.shape[1:]
    for c in range(group):
        dsend[c] = dec_term[0:var_rows, c * lanes : (c + 1) * lanes].astype(BF16)

    def plane_copies(i):
        to, ens, space = plane_place(i)
        row = lax.rem(to, inner)
        return (
            (
                remote(dsend.at[to], drecv.at[mine], d_s.at[to], d_r.at[mine], ens, space),
                remote(dsend.at[to], drecv.at[to], d_s.at[to], d_r.at[to], ens, space),
            ),
            (
                remote(csend.at[row], crecv.at[mine], c_s.at[to], c_r.at[mine], ens, space),
                remote(csend.at[row], crecv.at[to], c_s.at[to], c_r.at[to], ens, space),
            ),
            (
                remote(agsend, dall.at[mine], a_s.at[to], a_r.at[mine], ens, space),
                remote(agsend, dall.at[to], a_s.at[to], a_r.at[to], ens, space),
            ),
        )

    def outer_copies(i):
        to, ens, space = outer_place(i)
        return (
            (
                remote(zsend, zrecv.at[ring], z_s.at[to], z_r.at[ring], ens, space),
                remote(zsend, zrecv.at[to], z_s.at[to], z_r.at[to], ens, space),
            ),
            (
                remote(fsend.at[to], frecv.at[ring], f_s.at[to], f_r.at[ring], ens, space),
                remote(fsend.at[to], frecv.at[to], f_s.at[to], f_r.at[to], ens, space),
            ),
        )

    def each(count, copies, which, method, side):
        @pl.loop(1, count)
        def _(i):
            getattr(copies(i)[which][side], method)()

    each(group, plane_copies, 0, "start", 0)
    drecv[mine] = dsend[mine]
    grad_states = dot(q_rows, decp[...]).astype(BF16)
    gs_ref[...] = grad_states
    go[...] = dot(grad_states, ow_ref[...], NT).astype(BF16)

    for slot, shift, present in sides:
        for item in range(2):
            under(present, kv_copies(slot, shift, item)[1].wait_recv)

    @pl.loop(0, pairs)
    def _(p):
        columns = columns_of(p)
        scores = dot(scaled_queries(columns), extended(0, k_ref, columns), NT)
        if blocks == 1:
            scores = jnp.where(inside_rows[0], scores, MASKED_SCORE)
        else:
            scores = jnp.concatenate(
                [
                    jnp.where(
                        inside_rows[i % blocks],
                        scores[i * BLOCK : (i + 1) * BLOCK],
                        MASKED_SCORE,
                    )
                    for i in range(blocks * heads_per)
                ],
                axis=0,
            )
        exponent = jnp.exp(scores - jnp.max(scores, axis=-1, keepdims=True))
        attn_prob = exponent * (1.0 / jnp.sum(exponent, axis=-1, keepdims=True))
        prob[p] = attn_prob
        ao[:, columns] = merge_heads(
            dot(attn_prob.astype(BF16), extended(1, v_ref, columns))
        ).astype(BF16)

    wo_rows = fsend.shape[1]
    wo_term = dot(ao[...], q_rows, TN)
    for c in range(inner):
        for o in range(outer):
            top = (o * inner + c) * wo_rows
            csend[c, o * wo_rows : (o + 1) * wo_rows] = wo_term[top : top + wo_rows].astype(BF16)
    crecv[mine] = csend[seat]

    each(group, plane_copies, 0, "wait_recv", 1)
    dec_plane = jnp.sum(drecv[...].astype(F32), axis=0).astype(BF16)
    zsend[...] = dec_plane
    zrecv[ring] = dec_plane
    each(outer, outer_copies, 0, "start", 0)
    each(group, plane_copies, 1, "start", 0)

    def border_copies(p, slot, shift):
        out = remote(
            bsend.at[slot, p],
            brecv.at[1 - slot, p],
            b_s.at[slot, p],
            b_r.at[1 - slot, p],
            e,
            s + shift,
        )
        back = remote(
            bsend.at[slot, p], brecv.at[slot, p], b_s.at[slot, p], b_r.at[slot, p], e, s + shift
        )
        return out, back

    @pl.loop(0, pairs)
    def _(p):
        columns = columns_of(p)
        grads = split_heads(go[:, columns])
        attn_prob = prob[p]
        grad_prob = dot(grads, extended(1, v_ref, columns), NT)
        row_delta = jnp.sum(attn_prob * grad_prob, axis=-1, keepdims=True)
        grad_scores = (attn_prob * (grad_prob - row_delta)).astype(BF16)
        value_term = dot(attn_prob.astype(BF16), grads, TN)
        key_term = dot(grad_scores, scaled_queries(columns), TN)
        for item, term, mid in ((0, key_term, kmid), (1, value_term, vmid)):
            bsend[0, p, item] = term[0:nodes].astype(BF16)
            bsend[1, p, item] = term[2 * nodes :].astype(BF16)
            mid[:, columns] = term[nodes : 2 * nodes]
        for slot, shift, present in sides:
            under(present, border_copies(p, slot, shift)[0].start)
        gq_ref[:, columns] = (
            merge_heads(dot(grad_scores, extended(0, k_ref, columns))) * scale
        ).astype(BF16)

    each(outer, outer_copies, 0, "wait_recv", 1)
    dec_sum = jnp.sum(zrecv[...].astype(F32), axis=0).astype(BF16)
    agsend[...] = dec_sum
    dall[mine] = dec_sum
    each(group, plane_copies, 2, "start", 0)

    each(group, plane_copies, 1, "wait_recv", 1)
    wo_plane = jnp.sum(crecv[...].astype(F32), axis=0).astype(BF16)
    for o in range(outer):
        fsend[o] = wo_plane[o * wo_rows : (o + 1) * wo_rows]
    frecv[ring] = fsend[ring]
    each(outer, outer_copies, 1, "start", 0)

    @pl.loop(0, pairs)
    def _(p):
        columns = columns_of(p)
        for slot, shift, present in sides:
            under(present, border_copies(p, slot, shift)[1].wait_recv)
        for item, mid, out_ref in ((0, kmid, gk_ref), (1, vmid, gv_ref)):
            out_ref[:, columns] = (
                mid[:, columns]
                + brecv[0, p, item].astype(F32)
                + brecv[1, p, item].astype(F32)
            ).astype(BF16)

    each(outer, outer_copies, 1, "wait_recv", 1)
    wo_sum = jnp.sum(frecv[...].astype(F32), axis=0)
    gwo_ref[...] = dot(wo_sum.astype(BF16), decp[...])

    each(group, plane_copies, 2, "wait_recv", 1)
    for c in range(group):
        gdec_ref[:, c * lanes : (c + 1) * lanes] = dall[c].astype(F32)[0:n_var]

    for out, _, present in t_copies():
        under(present, out.wait_send)
    for slot, shift, present in sides:
        for item in range(2):
            under(present, kv_copies(slot, shift, item)[0].wait_send)
        under(present, q_copies(slot, shift)[0].wait_send)

        def drain():
            @pl.loop(0, pairs)
            def _(p):
                border_copies(p, slot, shift)[0].wait_send()

        under(present, drain)

    for which in range(3):
        each(group, plane_copies, which, "wait_send", 0)
    for which in range(2):
        each(outer, outer_copies, which, "wait_send", 0)


def hand_over(*refs):
    half = len(refs) // 2
    for source, result in zip(refs[:half], refs[half:]):
        result[...] = source[...]


def per_device(
    node_states,
    query,
    key,
    value,
    out_weight,
    dec_weight,
    target,
    area_weight,
    var_weight,
    edges,
    edge_weight,
    windows,
):
    n_e, n_s = lax.axis_size("ens"), lax.axis_size("space")
    inner = math.gcd(n_s, INNER)
    outer, group = n_s // inner, n_e * inner
    nodes, width = node_states.shape[1:]
    att = query.shape[2]
    n_var, points = target.shape
    pairs = att // LANES
    var_pad = -(-n_var // LANES) * LANES
    var_rows = -(-n_var // 16) * 16
    lanes = width // group
    wo_rows = att // n_s
    span = 3 * nodes
    heads_per = LANES // HEAD_DIM
    dma = pltpu.SemaphoreType.DMA
    operands = (
        node_states[0],
        query[0],
        key[0],
        value[0],
        out_weight,
        dec_weight,
        target,
        area_weight[None, :],
        var_weight[None, :],
        edges,
        edge_weight,
        windows.T,
    )
    outs = pl.pallas_call(
        functools.partial(kernel, n_e, n_s),
        out_shape=(
            jax.ShapeDtypeStruct((nodes, width), BF16),
            jax.ShapeDtypeStruct((nodes, att), BF16),
            jax.ShapeDtypeStruct((nodes, att), BF16),
            jax.ShapeDtypeStruct((nodes, att), BF16),
            jax.ShapeDtypeStruct((wo_rows, width), F32),
            jax.ShapeDtypeStruct((n_var, width), F32),
        ),
        in_specs=[pl.BlockSpec(memory_space=pltpu.HBM)] * len(operands),
        out_specs=[pl.BlockSpec(memory_space=pltpu.VMEM)] * 6,
        scratch_shapes=[pltpu.VMEM(x.shape, x.dtype) for x in operands]
        + [
            pltpu.VMEM((var_pad, width), BF16),
            pltpu.VMEM((span, points), BF16),
            pltpu.VMEM((2, 2, nodes, att), BF16),
            pltpu.VMEM((var_pad, nodes), BF16),
            pltpu.VMEM((n_e, 3, var_pad, nodes), BF16),
            pltpu.VMEM((var_pad, points), BF16),
            pltpu.VMEM((2, var_pad, nodes), BF16),
            pltpu.VMEM((2, var_pad, nodes), BF16),
            pltpu.VMEM((pairs, heads_per * nodes, span), F32),
            pltpu.VMEM((nodes, att), BF16),
            pltpu.VMEM((nodes, att), BF16),
            pltpu.VMEM((nodes, att), F32),
            pltpu.VMEM((nodes, att), F32),
            pltpu.VMEM((2, pairs, 2, nodes, LANES), BF16),
            pltpu.VMEM((2, pairs, 2, nodes, LANES), BF16),
            pltpu.VMEM((inner, outer * wo_rows, var_pad), BF16),
            pltpu.VMEM((group, outer * wo_rows, var_pad), BF16),
            pltpu.VMEM((group, var_rows, lanes), BF16),
            pltpu.VMEM((group, var_rows, lanes), BF16),
            pltpu.VMEM((var_rows, lanes), BF16),
            pltpu.VMEM((outer, var_rows, lanes), BF16),
            pltpu.VMEM((outer, wo_rows, var_pad), BF16),
            pltpu.VMEM((outer, wo_rows, var_pad), BF16),
            pltpu.VMEM((var_rows, lanes), BF16),
            pltpu.VMEM((group, var_rows, lanes), BF16),
            dma((2, 2)),
            dma((2, 2)),
            dma((n_e, 3)),
            dma((n_e, 3)),
            dma((2,)),
            dma((2,)),
            dma((2, pairs)),
            dma((2, pairs)),
            dma((group,)),
            dma((group,)),
            dma((group,)),
            dma((group,)),
            dma((group,)),
            dma((group,)),
            dma((outer,)),
            dma((outer,)),
            dma((outer,)),
            dma((outer,)),
            dma((len(operands),)),
        ],
        compiler_params=pltpu.CompilerParams(
            collective_id=0, has_side_effects=True, vmem_limit_bytes=67_043_328
        ),
    )(*operands)
    outs = pl.pallas_call(
        hand_over,
        out_shape=[jax.ShapeDtypeStruct(x.shape, x.dtype) for x in outs],
        in_specs=[pl.BlockSpec(memory_space=pltpu.VMEM)] * len(outs),
        out_specs=[pl.BlockSpec(memory_space=pltpu.VMEM)] * len(outs),
        compiler_params=pltpu.CompilerParams(vmem_limit_bytes=67_043_328),
    )(*outs)
    grad_states, grad_query, grad_key, grad_value, grad_wo, grad_dec = outs
    return (
        grad_states[None],
        grad_query[None],
        grad_key[None],
        grad_value[None],
        grad_wo,
        grad_dec,
    )


def solution(mesh):
    banded = P("ens", "space", None)
    in_specs = (
        banded,
        banded,
        banded,
        banded,
        P(),
        P(),
        P(None, "space"),
        P("space"),
        P(),
        P(None, "space"),
        P(None, "space"),
        P(None, "space"),
    )
    out_specs = (banded, banded, banded, banded, P("space", None), P())
    return jax.shard_map(
        per_device, mesh=mesh, in_specs=in_specs, out_specs=out_specs, check_vma=False
    )
```

profile of v0, /device:TPU:1, one launch (start us, length us, event | category | flops | bytes accessed | tf_op | source)
XLA Modules:
  0.0 37.9 jit_solution(2295356337173937534)
XLA Ops:
  0.6 34.9 %shard_map.163 = (bf16[128,1024]{1,0:T(8,128)(2,1)}, bf16[128,512]{1,0:T(8,128)(2,1)}, bf16[128,512]{1,0:T(8,128)(2,1)}, bf16[128,512]{1,0:T(8,128)(2,1)}, f32[32,1024]{1,0:T(8,128)}, /*index=5*/f32[100,1024]{1,0:T(8,128)}) custom-call(bf16[128,1024]{1,0:T(8,128)(2,1)} %bitcast.11, bf16[128,512]{1,0:T(8,128)(2,1)} %bitcast.12, bf16[128,512]{1,0:T(8,128)(2,1)} %bitcast.13, ...), custom_call_target="tpu_custom_call" | custom-call | tf_op jit(solution)/shard_map/pallas_call | solution.py:575
  35.6 2.3 %shard_map.164 = (bf16[128,1024]{1,0:T(8,128)(2,1)}, bf16[128,512]{1,0:T(8,128)(2,1)}, bf16[128,512]{1,0:T(8,128)(2,1)}, bf16[128,512]{1,0:T(8,128)(2,1)}, f32[32,1024]{1,0:T(8,128)}, /*index=5*/f32[100,1024]{1,0:T(8,128)}) custom-call(bf16[128,1024]{1,0:T(8,128)(2,1)} %get-tuple-element.18.refs_0_, bf16[128,512]{1,0:T(8,128)(2,1)} %get-tuple-element.19.refs_1_, ...), custom_call_target="tpu_custom_call" | custom-call | tf_op jit(solution)/shard_map/pallas_call | solution.py:638
where the time goes:
time: 38.6 us; the launch traced here: 37.9 us
  Pallas kernels  37.3 us (97%)
  between operations  0.64 us (2%)
    pallas_call x1, Pallas kernels, per_device(): pl.pallas_call(functools.partial(kernel, n_e, n_s), out_shape=(jax.ShapeD...  34.9 us
    pallas_call x1, Pallas kernels, per_device(): pl.pallas_call(hand_over, out_shape=[jax.ShapeDtypeStruct(x.shape, x.dtyp...  2.33 us

commit v1 on v0

v1 whole, which is shorter than its diff:
```python
import functools
import math

import jax
import jax.numpy as jnp
from jax import lax
from jax.experimental import pallas as pl
from jax.experimental.pallas import tpu as pltpu
from jax.sharding import PartitionSpec as P

HEAD_DIM = 64
BLOCK = 128
INNER = 4
LANES = 128
SMOOTH_SQUARE = 0.0625
MASKED_SCORE = -1e30
F32 = jnp.float32
BF16 = jnp.bfloat16
NT = (((1,), (1,)), ((), ()))
TN = (((0,), (0,)), ((), ()))


def smooth_slope(diff_value):
    return diff_value * lax.rsqrt(diff_value * diff_value + SMOOTH_SQUARE)


def dot(a, b, dims=(((1,), (0,)), ((), ()))):
    return lax.dot_general(a, b, dims, preferred_element_type=F32)


def kernel(
    n_e,
    n_s,
    states_hbm,
    q_hbm,
    k_hbm,
    v_hbm,
    ow_hbm,
    dec_hbm,
    target_hbm,
    area_hbm,
    var_hbm,
    edges_hbm,
    ew_hbm,
    win_hbm,
    gs_ref,
    gq_ref,
    gk_ref,
    gv_ref,
    gwo_ref,
    gdec_ref,
    states_ref,
    q_ref,
    k_ref,
    v_ref,
    ow_ref,
    dec_ref,
    target_ref,
    area_ref,
    var_ref,
    edges_ref,
    ew_ref,
    win_ref,
    decp,
    mix,
    wt,
    kh,
    text,
    gp,
    qsend,
    qrecv,
    qs,
    prob,
    ao,
    go,
    kmid,
    vmid,
    bsend,
    brecv,
    csend,
    crecv,
    dsend,
    drecv,
    zsend,
    zrecv,
    fsend,
    frecv,
    agsend,
    dall,
    kv_s,
    kv_r,
    t_s,
    t_r,
    q_s,
    q_r,
    b_s,
    b_r,
    c_s,
    c_r,
    d_s,
    d_r,
    a_s,
    a_r,
    z_s,
    z_r,
    f_s,
    f_r,
    load_sem,
    hello_sem,
):
    e = lax.axis_index("ens")
    s = lax.axis_index("space")
    inner = math.gcd(n_s, INNER)
    outer = n_s // inner
    group = n_e * inner
    ring, seat = lax.div(s, inner), lax.rem(s, inner)
    mine = e * inner + seat
    nodes, width = states_ref.shape
    att = q_ref.shape[1]
    pairs = att // LANES
    n_var = dec_ref.shape[0]
    points = target_ref.shape[1]
    scale = 1.0 / math.sqrt(HEAD_DIM)
    has_left = s > 0
    has_right = s < n_s - 1
    sides = ((0, -1, has_left), (1, 1, has_right))
    rings = ((0, -1, ring > 0), (1, 1, ring < outer - 1))

    def remote(src, dst, send_sem, recv_sem, ens, space):
        return pltpu.make_async_remote_copy(
            src_ref=src,
            dst_ref=dst,
            send_sem=send_sem,
            recv_sem=recv_sem,
            device_id=(ens, space),
            device_id_type=pl.DeviceIdType.MESH,
        )

    def received(dst, sem):
        remote(dst, dst, sem, sem, e, s).wait_recv()

    def sent(src, sem):
        remote(src, src, sem, sem, e, s).wait_send()

    loads = {}
    for i, (name, source, held) in enumerate(
        (
            ("states", states_hbm, states_ref),
            ("dec", dec_hbm, dec_ref),
            ("edges", edges_hbm, edges_ref),
            ("ew", ew_hbm, ew_ref),
            ("k", k_hbm, k_ref),
            ("v", v_hbm, v_ref),
            ("target", target_hbm, target_ref),
            ("area", area_hbm, area_ref),
            ("var", var_hbm, var_ref),
            ("win", win_hbm, win_ref),
            ("ow", ow_hbm, ow_ref),
            ("q", q_hbm, q_ref),
        )
    ):
        loads[name] = pltpu.make_async_copy(source, held, load_sem.at[i])

    def loaded(*wanted):
        for name in wanted:
            loads[name].wait()

    for load in loads.values():
        load.start()

    barrier = pltpu.get_barrier_semaphore()

    def under(present, action):
        if present is None:
            action()
        else:
            pl.when(present)(action)

    def signal(semaphore, ens, space):
        pl.semaphore_signal(
            semaphore,
            inc=1,
            device_id=(ens, space),
            device_id_type=pl.DeviceIdType.MESH,
        )

    near = [
        (lax.rem(e + r, n_e), s + shift, present)
        for shift, present in ((-1, has_left), (1, has_right), (0, None))
        for r in range(n_e)
        if r or shift
    ] + [(e, s + shift * inner, present) for _, shift, present in rings if inner > 1]

    for ens, space, present in near:
        under(present, functools.partial(signal, barrier, ens, space))

    def hello():
        for side, shift, present in rings:
            under(
                present,
                functools.partial(signal, hello_sem.at[1 - side], e, s + shift * inner),
            )

    def hello_wait():
        for side, _, present in rings:
            under(present, functools.partial(pl.semaphore_wait, hello_sem.at[side], 1))

    for slot, _, present in sides:

        @pl.when(jnp.logical_not(present))
        def _():
            kh[slot] = jnp.zeros(kh.shape[1:], BF16)
            text[2 * slot] = jnp.zeros(text.shape[1:], BF16)
            qrecv[slot] = jnp.zeros(qrecv.shape[1:], BF16)
            brecv[slot] = jnp.zeros(brecv.shape[1:], BF16)

    decp[...] = jnp.zeros(decp.shape, BF16)
    loaded("states", "dec")
    decp[0:n_var, :] = dec_ref[...]
    text[1, e] = dot(decp[...], states_ref[...], NT).astype(BF16)
    peers = sum(1 if present is None else present.astype(jnp.int32) for _, _, present in near)
    pl.semaphore_wait(barrier, peers)

    for r in range(n_e):
        ens = lax.rem(e + r, n_e)
        for shift, present in ((-1, has_left), (1, has_right), (0, None)):
            if r or shift:
                out = remote(
                    text.at[1, e],
                    text.at[1 - shift, e],
                    t_s.at[1 + shift],
                    t_r.at[1 - shift],
                    ens,
                    s + shift,
                )
                under(present, out.start)
    if outer > 2:
        hello()

    def kv_copy(slot, shift, item):
        return remote(
            k_ref if item == 0 else v_ref,
            kh.at[1 - slot, item],
            kv_s.at[slot],
            kv_r.at[1 - slot],
            e,
            s + shift,
        )

    def start_kv():
        for slot, shift, present in sides:
            for item in range(2):
                under(present, kv_copy(slot, shift, item).start)

    loaded("k", "v")
    start_kv()

    loaded("edges", "ew")
    first = (s - 1) * nodes
    chunk = nodes
    for part in range(3):
        node_ids = first + part * chunk + lax.broadcasted_iota(jnp.int32, (chunk, points), 0)
        total = jnp.zeros((chunk, points), F32)
        for slot in range(edges_ref.shape[0]):
            total = total + jnp.where(
                node_ids == edges_ref[slot : slot + 1, :], ew_ref[slot : slot + 1, :], 0.0
            )
        wt[part * chunk : (part + 1) * chunk, :] = total.astype(BF16)

    loaded("target", "area", "var", "win", "q", "ow")
    mix[...] = dot(decp[...], ow_ref[...], NT).astype(BF16)

    if n_e > 1:
        received(text.at[1, pl.ds(0, n_e - 1)], t_r.at[1])
    for slot, _, present in sides:
        under(present, functools.partial(received, text.at[2 * slot], t_r.at[2 * slot]))
    if outer > 2:
        hello_wait()
    if outer > 3:
        hello()

    def predictions(member):
        cat = jnp.concatenate([text[i, member] for i in range(3)], axis=1)
        return dot(cat, wt[...])[0:n_var].astype(BF16).astype(F32)

    own_pred = predictions(e)
    slopes = smooth_slope(own_pred - target_ref[...])
    pair_sum = jnp.zeros_like(own_pred)
    for r in range(1, n_e):
        pair_sum = pair_sum + smooth_slope(own_pred - predictions(lax.rem(e + r, n_e)))
    slopes = slopes - pair_sum / (n_e - 1)
    square = (n_var, n_var)
    diagonal = lax.broadcasted_iota(jnp.int32, square, 0) == lax.broadcasted_iota(
        jnp.int32, square, 1
    )
    var_column = jnp.sum(jnp.where(diagonal, var_ref[...], 0.0), axis=1, keepdims=True)
    gp[...] = jnp.zeros(gp.shape, BF16)
    gp[0:n_var, :] = (area_ref[...] * var_column * slopes).astype(BF16)
    q_ext = dot(gp[...], wt[...], NT)
    qsend[0] = q_ext[:, 0:nodes].astype(BF16)
    qsend[1] = q_ext[:, 2 * nodes :].astype(BF16)

    for slot, shift, present in sides:
        out = remote(
            qsend.at[slot], qrecv.at[1 - slot], q_s.at[slot], q_r.at[1 - slot], e, s + shift
        )
        under(present, out.start)

    blocks = win_ref.shape[0]
    key_place = first + lax.broadcasted_iota(jnp.int32, (1, 3 * nodes), 1)
    inside_rows = [
        (key_place >= win_ref[b : b + 1, 0:1]) & (key_place < win_ref[b : b + 1, 1:2])
        for b in range(blocks)
    ]
    heads_per = LANES // HEAD_DIM
    lane_head = lax.broadcasted_iota(jnp.int32, (nodes, LANES), 1) // HEAD_DIM

    def split_heads(x):
        x = x.astype(F32)
        return jnp.concatenate(
            [jnp.where(lane_head == h, x, 0.0).astype(BF16) for h in range(heads_per)], axis=0
        )

    def merge_heads(x):
        out = x[0:nodes]
        for h in range(1, heads_per):
            out = jnp.where(lane_head == h, x[h * nodes : (h + 1) * nodes], out)
        return out

    def extended(item, own_ref, columns):
        return jnp.concatenate(
            [kh[0, item, :, columns], own_ref[:, columns], kh[1, item, :, columns]], axis=0
        )

    def columns_of(p):
        return slice(p * LANES, (p + 1) * LANES)

    for p in range(pairs):
        qs[p] = split_heads(q_ref[:, columns_of(p)].astype(F32) * scale)

    for slot, _, present in sides:
        under(present, functools.partial(received, qrecv.at[slot], q_r.at[slot]))
    q_own = q_ext[:, nodes : 2 * nodes] + qrecv[0].astype(F32) + qrecv[1].astype(F32)
    q_rows = q_own.T.astype(BF16)
    dec_term = dot(q_own.astype(BF16), states_ref[...])
    var_rows, lanes = dsend.shape[1:]
    for c in range(group):
        dsend[c] = dec_term[0:var_rows, c * lanes : (c + 1) * lanes].astype(BF16)

    def plane_start(which):
        @pl.loop(1, group)
        def _(i):
            to = lax.rem(mine + i, group)
            ens, row = lax.div(to, inner), lax.rem(to, inner)
            source, target, s_sem, r_sem = (
                (dsend.at[to], drecv.at[mine], d_s, d_r),
                (csend.at[row], crecv.at[mine], c_s, c_r),
                (agsend, dall.at[mine], a_s, a_r),
            )[which]
            remote(source, target, s_sem, r_sem, ens, ring * inner + row).start()

    def outer_start(which):
        @pl.loop(1, outer)
        def _(i):
            to = lax.rem(ring + i, outer)
            source, target, s_sem, r_sem = (
                (zsend, zrecv.at[ring], z_s, z_r),
                (fsend.at[to], frecv.at[ring], f_s, f_r),
            )[which]
            remote(source, target, s_sem, r_sem, e, to * inner + seat).start()

    plane_start(0)
    for slot, _, present in sides:
        under(present, functools.partial(received, kh.at[slot], kv_r.at[slot]))

    for p in range(pairs):
        columns = columns_of(p)
        scores = dot(qs[p], extended(0, k_ref, columns), NT)
        if blocks == 1:
            scores = jnp.where(inside_rows[0], scores, MASKED_SCORE)
        else:
            scores = jnp.concatenate(
                [
                    jnp.where(
                        inside_rows[i % blocks],
                        scores[i * BLOCK : (i + 1) * BLOCK],
                        MASKED_SCORE,
                    )
                    for i in range(blocks * heads_per)
                ],
                axis=0,
            )
        exponent = jnp.exp(scores - jnp.max(scores, axis=-1, keepdims=True))
        attn_prob = exponent * (1.0 / jnp.sum(exponent, axis=-1, keepdims=True))
        prob[p] = attn_prob
        ao[:, columns] = merge_heads(
            dot(attn_prob.astype(BF16), extended(1, v_ref, columns))
        ).astype(BF16)

    wo_rows = fsend.shape[1]
    wo_term = dot(ao[...], q_rows, TN)
    for c in range(inner):
        for o in range(outer):
            top = (o * inner + c) * wo_rows
            csend[c, o * wo_rows : (o + 1) * wo_rows] = wo_term[top : top + wo_rows].astype(BF16)
    plane_start(1)
    drecv[mine] = dsend[mine]
    crecv[mine] = csend[seat]
    go[...] = dot(q_rows, mix[...]).astype(BF16)

    for p in range(pairs):
        columns = columns_of(p)
        grads = split_heads(go[:, columns])
        attn_prob = prob[p]
        grad_prob = dot(grads, extended(1, v_ref, columns), NT)
        row_delta = jnp.sum(attn_prob * grad_prob, axis=-1, keepdims=True)
        grad_scores = (attn_prob * (grad_prob - row_delta)).astype(BF16)
        value_term = dot(attn_prob.astype(BF16), grads, TN)
        key_term = dot(grad_scores, qs[p], TN)
        for item, term, mid in ((0, key_term, kmid), (1, value_term, vmid)):
            bsend[0, p, item] = term[0:nodes].astype(BF16)
            bsend[1, p, item] = term[2 * nodes :].astype(BF16)
            mid[:, columns] = term[nodes : 2 * nodes]
        for slot, shift, present in sides:
            out = remote(
                bsend.at[slot, p],
                brecv.at[1 - slot, p],
                b_s.at[slot],
                b_r.at[1 - slot],
                e,
                s + shift,
            )
            under(present, out.start)
        gq_ref[:, columns] = (
            merge_heads(dot(grad_scores, extended(0, k_ref, columns))) * scale
        ).astype(BF16)

    gs_ref[...] = dot(q_rows, decp[...]).astype(BF16)
    received(drecv.at[pl.ds(0, group - 1)], d_r)
    dec_plane = jnp.sum(drecv[...].astype(F32), axis=0).astype(BF16)
    zsend[...] = dec_plane
    zrecv[ring] = dec_plane
    if outer > 3:
        hello_wait()
    for _ in range(outer - 4):
        hello()
        hello_wait()
    outer_start(0)

    received(crecv.at[pl.ds(0, group - 1)], c_r)
    wo_plane = jnp.sum(crecv[...].astype(F32), axis=0).astype(BF16)
    for o in range(outer):
        fsend[o] = wo_plane[o * wo_rows : (o + 1) * wo_rows]
    frecv[ring] = fsend[ring]
    outer_start(1)

    if outer > 1:
        received(zrecv.at[pl.ds(0, outer - 1)], z_r)
    dec_sum = jnp.sum(zrecv[...].astype(F32), axis=0).astype(BF16)
    agsend[...] = dec_sum
    dall[mine] = dec_sum
    plane_start(2)

    for slot, _, present in sides:
        under(present, functools.partial(received, brecv.at[slot], b_r.at[slot]))
    for p in range(pairs):
        columns = columns_of(p)
        for item, mid, out_ref in ((0, kmid, gk_ref), (1, vmid, gv_ref)):
            out_ref[:, columns] = (
                mid[:, columns]
                + brecv[0, p, item].astype(F32)
                + brecv[1, p, item].astype(F32)
            ).astype(BF16)

    if outer > 1:
        received(frecv.at[pl.ds(0, outer - 1)], f_r)
    wo_sum = jnp.sum(frecv[...].astype(F32), axis=0)
    gwo_ref[...] = dot(wo_sum.astype(BF16), decp[...])

    for slot, shift, present in sides:

        def drain():
            for _ in range(n_e):
                sent(text.at[1, 0], t_s.at[1 + shift])
            sent(kh.at[slot], kv_s.at[slot])
            sent(qsend.at[slot], q_s.at[slot])
            sent(bsend.at[slot], b_s.at[slot])

        under(present, drain)
    if n_e > 1:
        sent(text.at[1, pl.ds(0, n_e - 1)], t_s.at[1])
    sent(dsend.at[pl.ds(0, group - 1)], d_s)
    sent(crecv.at[pl.ds(0, group - 1)], c_s)
    if outer > 1:
        sent(zrecv.at[pl.ds(0, outer - 1)], z_s)
        sent(frecv.at[pl.ds(0, outer - 1)], f_s)
    received(dall.at[pl.ds(0, group - 1)], a_r)
    for c in range(group):
        gdec_ref[:, c * lanes : (c + 1) * lanes] = dall[c].astype(F32)[0:n_var]
    sent(dall.at[pl.ds(0, group - 1)], a_s)


def hand_over(*refs):
    count = (len(refs) - 1) // 2
    sems = refs[-1]
    copies = [
        pltpu.make_async_copy(refs[i], refs[count + i], sems.at[i]) for i in range(count)
    ]
    for copy in copies:
        copy.start()
    for copy in copies:
        copy.wait()


def per_device(
    node_states,
    query,
    key,
    value,
    out_weight,
    dec_weight,
    target,
    area_weight,
    var_weight,
    edges,
    edge_weight,
    windows,
):
    n_e, n_s = lax.axis_size("ens"), lax.axis_size("space")
    inner = math.gcd(n_s, INNER)
    outer, group = n_s // inner, n_e * inner
    nodes, width = node_states.shape[1:]
    att = query.shape[2]
    n_var, points = target.shape
    pairs = att // LANES
    var_pad = -(-n_var // LANES) * LANES
    var_rows = -(-n_var // 16) * 16
    lanes = width // group
    wo_rows = att // n_s
    span = 3 * nodes
    heads_per = LANES // HEAD_DIM
    dma = pltpu.SemaphoreType.DMA
    operands = (
        node_states[0],
        query[0],
        key[0],
        value[0],
        out_weight,
        dec_weight,
        target,
        area_weight[None, :],
        var_weight[None, :],
        edges,
        edge_weight,
        windows.T,
    )
    outs = pl.pallas_call(
        functools.partial(kernel, n_e, n_s),
        out_shape=(
            pltpu.VMEM((nodes, width), BF16),
            pltpu.VMEM((nodes, att), BF16),
            pltpu.VMEM((nodes, att), BF16),
            pltpu.VMEM((nodes, att), BF16),
            pltpu.VMEM((wo_rows, width), F32),
            pltpu.VMEM((n_var, width), F32),
        ),
        in_specs=[pl.BlockSpec(memory_space=pltpu.HBM)] * len(operands),
        out_specs=[pl.BlockSpec(memory_space=pltpu.VMEM)] * 6,
        scratch_shapes=[pltpu.VMEM(x.shape, x.dtype) for x in operands]
        + [
            pltpu.VMEM((var_pad, width), BF16),
            pltpu.VMEM((var_pad, att), BF16),
            pltpu.VMEM((span, points), BF16),
            pltpu.VMEM((2, 2, nodes, att), BF16),
            pltpu.VMEM((3, n_e, var_pad, nodes), BF16),
            pltpu.VMEM((var_pad, points), BF16),
            pltpu.VMEM((2, var_pad, nodes), BF16),
            pltpu.VMEM((2, var_pad, nodes), BF16),
            pltpu.VMEM((pairs, heads_per * nodes, LANES), BF16),
            pltpu.VMEM((pairs, heads_per * nodes, span), F32),
            pltpu.VMEM((nodes, att), BF16),
            pltpu.VMEM((nodes, att), BF16),
            pltpu.VMEM((nodes, att), F32),
            pltpu.VMEM((nodes, att), F32),
            pltpu.VMEM((2, pairs, 2, nodes, LANES), BF16),
            pltpu.VMEM((2, pairs, 2, nodes, LANES), BF16),
            pltpu.VMEM((inner, outer * wo_rows, var_pad), BF16),
            pltpu.VMEM((group, outer * wo_rows, var_pad), BF16),
            pltpu.VMEM((group, var_rows, lanes), BF16),
            pltpu.VMEM((group, var_rows, lanes), BF16),
            pltpu.VMEM((var_rows, lanes), BF16),
            pltpu.VMEM((outer, var_rows, lanes), BF16),
            pltpu.VMEM((outer, wo_rows, var_pad), BF16),
            pltpu.VMEM((outer, wo_rows, var_pad), BF16),
            pltpu.VMEM((var_rows, lanes), BF16),
            pltpu.VMEM((group, var_rows, lanes), BF16),
            dma((2,)),
            dma((2,)),
            dma((3,)),
            dma((3,)),
            dma((2,)),
            dma((2,)),
            dma((2,)),
            dma((2,)),
            dma,
            dma,
            dma,
            dma,
            dma,
            dma,
            dma,
            dma,
            dma,
            dma,
            dma((len(operands),)),
            pltpu.SemaphoreType.REGULAR((2,)),
        ],
        compiler_params=pltpu.CompilerParams(
            collective_id=0, has_side_effects=True, vmem_limit_bytes=40_000_000
        ),
    )(*(pltpu.with_memory_space_constraint(x, pltpu.HBM) for x in operands))
    outs = pl.pallas_call(
        hand_over,
        out_shape=[jax.ShapeDtypeStruct(x.shape, x.dtype) for x in outs],
        in_specs=[pl.BlockSpec(memory_space=pltpu.VMEM)] * len(outs),
        out_specs=[pl.BlockSpec(memory_space=pltpu.HBM)] * len(outs),
        scratch_shapes=[dma((len(outs),))],
        compiler_params=pltpu.CompilerParams(vmem_limit_bytes=20_000_000),
    )(*outs)
    grad_states, grad_query, grad_key, grad_value, grad_wo, grad_dec = outs
    return (
        grad_states[None],
        grad_query[None],
        grad_key[None],
        grad_value[None],
        grad_wo,
        grad_dec,
    )


def solution(mesh):
    banded = P("ens", "space", None)
    in_specs = (
        banded,
        banded,
        banded,
        banded,
        P(),
        P(),
        P(None, "space"),
        P("space"),
        P(),
        P(None, "space"),
        P(None, "space"),
        P(None, "space"),
    )
    out_specs = (banded, banded, banded, banded, P("space", None), P())
    return jax.shard_map(
        per_device, mesh=mesh, in_specs=in_specs, out_specs=out_specs, check_vma=False
    )
```

time: 38.6 us -> 32.6 us (0.84)
  Pallas kernels: 37.3 us -> 31.4 us
    pallas_call x1, Pallas kernels: 34.9 us -> 30.3 us  [per_device(): pl.pallas_call(functools.partial(kernel, n_e, n_s), out_shape=(pltpu.VMEM...]
    pallas_call x1, Pallas kernels: 2.33 us -> 1.07 us  [per_device(): pl.pallas_call(hand_over, out_shape=[jax.ShapeDtypeStruct(x.shape, x.dtyp...]
where the time goes in v1:
time: 32.6 us; the launch traced here: 32.1 us
  Pallas kernels  31.4 us (96%)
  between operations  0.64 us (2%)
    pallas_call x1, Pallas kernels, per_device(): pl.pallas_call(functools.partial(kernel, n_e, n_s), out_shape=(pltpu.VMEM...  30.3 us
    pallas_call x1, Pallas kernels, per_device(): pl.pallas_call(hand_over, out_shape=[jax.ShapeDtypeStruct(x.shape, x.dtyp...  1.07 us

profile of v1, /device:TPU:1, one launch (start us, length us, event | category | flops | bytes accessed | tf_op | source)
XLA Modules:
  0.0 32.1 jit_solution(15457644582102651395)
XLA Ops:
  0.6 30.3 %shard_map.163 = (bf16[128,1024]{1,0:T(8,128)(2,1)S(1)}, bf16[128,512]{1,0:T(8,128)(2,1)S(1)}, bf16[128,512]{1,0:T(8,128)(2,1)S(1)}, bf16[128,512]{1,0:T(8,128)(...) custom-call(bf16[128,1024]{1,0:T(8,128)(2,1)} %bitcast.11, bf16[128,512]{1,0:T(8,128)(2,1)} %bitcast.12, ...), custom_call_target="tpu_custom_call" | custom-call | tf_op jit(solution)/shard_map/pallas_call | solution.py:557
  31.0 1.1 %shard_map.164 = (bf16[128,1024]{1,0:T(8,128)(2,1)}, bf16[128,512]{1,0:T(8,128)(2,1)}, bf16[128,512]{1,0:T(8,128)(2,1)}, bf16[128,512]{1,0:T(8,128)(2,1)}, f32[32,1024]{1,0:T(8,128)}, /*index=5*/f32[100,1024]{1,0:T(8,128)}) custom-call(bf16[128,1024]{1,0:T(8,128)(2,1)S(1)} %get-tuple-element.18.refs_0_, bf16[128,512]{1,0:T(8,128)(2,1)S(1)} %get-tuple-element.19.refs_1_, ...), custom_call_target="tpu_custom_call" | custom-call | tf_op jit(solution)/shard_map/pallas_call | solution.py:622

commit v2 on v1

--- a/solution.py
+++ b/solution.py
@@ -75,11 +75,21 @@
     go,
     kmid,
     vmid,
-    bsend,
-    brecv,
+    gsc,
+    qn,
+    rows_own,
+    rows_near,
+    slab,
+    stat,
+    stat_near,
+    go_near,
     csend,
+    cpair,
+    cmid,
     crecv,
     dsend,
+    dpair,
+    dmid,
     drecv,
     zsend,
     zrecv,
@@ -93,8 +103,12 @@
     t_r,
     q_s,
     q_r,
-    b_s,
-    b_r,
+    qn_s,
+    qn_r,
+    n_s_sem,
+    n_r_sem,
+    st_s,
+    st_r,
     c_s,
     c_r,
     d_s,
@@ -105,6 +119,12 @@
     z_r,
     f_s,
     f_r,
+    pd_s,
+    pd_r,
+    pc_s,
+    pc_r,
+    pa_s,
+    pa_r,
     load_sem,
     hello_sem,
 ):
@@ -114,7 +134,15 @@
     outer = n_s // inner
     group = n_e * inner
     ring, seat = lax.div(s, inner), lax.rem(s, inner)
-    mine = e * inner + seat
+    pair = math.gcd(inner, 2)
+    rows_in = inner // pair
+    half = group // pair
+    place, parity = lax.div(seat, pair), lax.rem(seat, pair)
+    mine = e * rows_in + place
+    spots = n_e * outer
+    everyone = half * outer
+    flat = drecv.shape[0] == everyone
+    seat_all = mine * outer + ring
     nodes, width = states_ref.shape
     att = q_ref.shape[1]
     pairs = att // LANES
@@ -212,7 +240,9 @@
             kh[slot] = jnp.zeros(kh.shape[1:], BF16)
             text[2 * slot] = jnp.zeros(text.shape[1:], BF16)
             qrecv[slot] = jnp.zeros(qrecv.shape[1:], BF16)
-            brecv[slot] = jnp.zeros(brecv.shape[1:], BF16)
+            qn[slot] = jnp.zeros(qn.shape[1:], BF16)
+            rows_near[slot] = jnp.zeros(rows_near.shape[1:], BF16)
+            stat_near[slot] = jnp.zeros(stat_near.shape[1:], F32)
 
     decp[...] = jnp.zeros(decp.shape, BF16)
     loaded("states", "dec")
@@ -234,26 +264,32 @@
                     s + shift,
                 )
                 under(present, out.start)
-    if outer > 2:
+    if outer > 1:
         hello()
 
     def kv_copy(slot, shift, item):
         return remote(
             k_ref if item == 0 else v_ref,
             kh.at[1 - slot, item],
-            kv_s.at[slot],
-            kv_r.at[1 - slot],
+            kv_s.at[slot, item],
+            kv_r.at[1 - slot, item],
             e,
             s + shift,
         )
 
-    def start_kv():
+    def to_sides(src, dst, s_sem, r_sem):
         for slot, shift, present in sides:
-            for item in range(2):
-                under(present, kv_copy(slot, shift, item).start)
+            out = remote(
+                src, dst.at[1 - slot], s_sem.at[slot], r_sem.at[1 - slot], e, s + shift
+            )
+            under(present, out.start)
+
+    def start_kv(item):
+        for slot, shift, present in sides:
+            under(present, kv_copy(slot, shift, item).start)
 
     loaded("k", "v")
-    start_kv()
+    start_kv(0)
 
     loaded("edges", "ew")
     first = (s - 1) * nodes
@@ -274,9 +310,8 @@
         received(text.at[1, pl.ds(0, n_e - 1)], t_r.at[1])
     for slot, _, present in sides:
         under(present, functools.partial(received, text.at[2 * slot], t_r.at[2 * slot]))
-    if outer > 2:
+    if outer > 1:
         hello_wait()
-    if outer > 3:
         hello()
 
     def predictions(member):
@@ -305,6 +340,7 @@
             qsend.at[slot], qrecv.at[1 - slot], q_s.at[slot], q_r.at[1 - slot], e, s + shift
         )
         under(present, out.start)
+    start_kv(1)
 
     blocks = win_ref.shape[0]
     key_place = first + lax.broadcasted_iota(jnp.int32, (1, 3 * nodes), 1)
@@ -338,41 +374,33 @@
     for p in range(pairs):
         qs[p] = split_heads(q_ref[:, columns_of(p)].astype(F32) * scale)
 
-    for slot, _, present in sides:
-        under(present, functools.partial(received, qrecv.at[slot], q_r.at[slot]))
-    q_own = q_ext[:, nodes : 2 * nodes] + qrecv[0].astype(F32) + qrecv[1].astype(F32)
-    q_rows = q_own.T.astype(BF16)
-    dec_term = dot(q_own.astype(BF16), states_ref[...])
-    var_rows, lanes = dsend.shape[1:]
-    for c in range(group):
-        dsend[c] = dec_term[0:var_rows, c * lanes : (c + 1) * lanes].astype(BF16)
-
-    def plane_start(which):
-        @pl.loop(1, group)
-        def _(i):
-            to = lax.rem(mine + i, group)
-            ens, row = lax.div(to, inner), lax.rem(to, inner)
-            source, target, s_sem, r_sem = (
-                (dsend.at[to], drecv.at[mine], d_s, d_r),
-                (csend.at[row], crecv.at[mine], c_s, c_r),
-                (agsend, dall.at[mine], a_s, a_r),
-            )[which]
-            remote(source, target, s_sem, r_sem, ens, ring * inner + row).start()
-
-    def outer_start(which):
-        @pl.loop(1, outer)
-        def _(i):
-            to = lax.rem(ring + i, outer)
-            source, target, s_sem, r_sem = (
-                (zsend, zrecv.at[ring], z_s, z_r),
-                (fsend.at[to], frecv.at[ring], f_s, f_r),
-            )[which]
-            remote(source, target, s_sem, r_sem, e, to * inner + seat).start()
-
-    plane_start(0)
-    for slot, _, present in sides:
-        under(present, functools.partial(received, kh.at[slot], kv_r.at[slot]))
-
+    def arrived(item):
+        for slot, _, present in sides:
+            under(present, functools.partial(received, kh.at[slot, item], kv_r.at[slot, item]))
+
+    arrived(0)
+    if outer > 2:
+        hello_wait()
+        hello()
+    heads_rows = heads_per * nodes
+    stat_lane = lax.broadcasted_iota(jnp.int32, (heads_rows, LANES), 1)
+
+    def put_stat(held, at, column):
+        return jnp.where(stat_lane == at, column, held)
+
+    stats = jnp.zeros((heads_rows, LANES), F32)
+    for bound in range(2):
+        edge = jnp.concatenate(
+            [
+                jnp.broadcast_to(
+                    win_ref[i % blocks : i % blocks + 1, bound : bound + 1].astype(F32),
+                    (BLOCK, 1),
+                )
+                for i in range(blocks * heads_per)
+            ],
+            axis=0,
+        )
+        stats = put_stat(stats, 3 * pairs + bound, edge)
     for p in range(pairs):
         columns = columns_of(p)
         scores = dot(qs[p], extended(0, k_ref, columns), NT)
@@ -390,90 +418,242 @@
                 ],
                 axis=0,
             )
-        exponent = jnp.exp(scores - jnp.max(scores, axis=-1, keepdims=True))
-        attn_prob = exponent * (1.0 / jnp.sum(exponent, axis=-1, keepdims=True))
-        prob[p] = attn_prob
+        row_max = jnp.max(scores, axis=-1, keepdims=True)
+        exponent = jnp.exp(scores - row_max)
+        inverse = 1.0 / jnp.sum(exponent, axis=-1, keepdims=True)
+        prob[p] = exponent * inverse
+        stats = put_stat(stats, p, row_max)
+        stats = put_stat(stats, pairs + p, inverse)
+
+    slab[...] = stats
+    if outer > 3:
+        hello_wait()
+        hello()
+    for slot, _, present in sides:
+        under(present, functools.partial(received, qrecv.at[slot], q_r.at[slot]))
+    q_own = q_ext[:, nodes : 2 * nodes] + qrecv[0].astype(F32) + qrecv[1].astype(F32)
+    q_rows = q_own.T.astype(BF16)
+    rows_own[...] = q_rows
+    dec_term = dot(q_own.astype(BF16), states_ref[...])
+    var_rows, lanes = dsend.shape[2:]
+    for c in range(group):
+        dsend[c // half, c % half] = dec_term[0:var_rows, c * lanes : (c + 1) * lanes].astype(BF16)
+
+    def pair_start(source, target, s_sem, r_sem):
+        if pair > 1:
+            remote(source, target, s_sem, r_sem, e, s + 1 - 2 * parity).start()
+
+    def plane_start(source, target, s_sem, r_sem):
+        @pl.loop(1, half)
+        def _(i):
+            to = lax.rem(mine + i, half)
+            ens, row = lax.div(to, rows_in), lax.rem(to, rows_in)
+            remote(
+                source if source is agsend else source.at[to],
+                target,
+                s_sem,
+                r_sem,
+                ens,
+                ring * inner + row * pair + parity,
+            ).start()
+
+    pair_start(dsend.at[1 - parity], dpair, pd_s, pd_r)
+    to_sides(rows_own, rows_near, n_s_sem, n_r_sem)
+    go[...] = dot(q_rows, mix[...]).astype(BF16)
+    if pair > 1:
+        received(dpair, pd_r)
+        dmid[...] = (dsend[parity].astype(F32) + dpair[...].astype(F32)).astype(BF16)
+    else:
+        dmid[...] = dsend[parity]
+    if outer > 1:
+        hello_wait()
+    for _ in range(outer - 4):
+        hello()
+        hello_wait()
+    if flat:
+        piece = drecv.shape[1]
+
+        def all_start(source_of, target, s_sem, r_sem):
+            for far in range(outer):
+                around = lax.rem(ring + far, outer)
+                for across in range(n_e):
+                    ens = lax.rem(e + across, n_e)
+                    for along in range(rows_in):
+                        if far or across or along:
+                            row = lax.rem(place + along, rows_in)
+                            remote(
+                                source_of(ens * rows_in + row, row, around),
+                                target,
+                                s_sem,
+                                r_sem,
+                                ens,
+                                around * inner + row * pair + parity,
+                            ).start()
+
+        def piece_rows(around):
+            return pl.ds(pl.multiple_of(around * piece, piece), piece)
+
+        all_start(
+            lambda member, row, around: dmid.at[member, piece_rows(around)],
+            drecv.at[seat_all],
+            d_s,
+            d_r,
+        )
+        drecv[seat_all] = dmid[mine, piece_rows(ring)]
+    else:
+        plane_start(dmid, drecv.at[mine], d_s, d_r)
+        drecv[mine] = dmid[mine]
+    arrived(1)
+    for p in range(pairs):
+        columns = columns_of(p)
         ao[:, columns] = merge_heads(
-            dot(attn_prob.astype(BF16), extended(1, v_ref, columns))
+            dot(prob[p].astype(BF16), extended(1, v_ref, columns))
         ).astype(BF16)
-
     wo_rows = fsend.shape[1]
     wo_term = dot(ao[...], q_rows, TN)
     for c in range(inner):
         for o in range(outer):
             top = (o * inner + c) * wo_rows
-            csend[c, o * wo_rows : (o + 1) * wo_rows] = wo_term[top : top + wo_rows].astype(BF16)
-    plane_start(1)
-    drecv[mine] = dsend[mine]
-    crecv[mine] = csend[seat]
-    go[...] = dot(q_rows, mix[...]).astype(BF16)
-
+            csend[c % pair, c // pair, o * wo_rows : (o + 1) * wo_rows] = wo_term[
+                top : top + wo_rows
+            ].astype(BF16)
+    pair_start(csend.at[1 - parity], cpair, pc_s, pc_r)
+    def wo_across():
+        if pair > 1:
+            received(cpair, pc_r)
+            cmid[...] = (csend[parity].astype(F32) + cpair[...].astype(F32)).astype(BF16)
+        else:
+            cmid[...] = csend[parity]
+
+        if flat:
+
+            def wo_part(around):
+                return pl.ds(pl.multiple_of(around * wo_rows, wo_rows), wo_rows)
+
+            all_start(
+                lambda member, row, around: cmid.at[row, wo_part(around)],
+                frecv.at[seat_all],
+                f_s,
+                f_r,
+            )
+            frecv[seat_all] = cmid[place, wo_part(ring)]
+            return
+
+        @pl.loop(1, rows_in)
+        def _(i):
+            to = lax.rem(place + i, rows_in)
+            remote(
+                cmid.at[to], crecv.at[place], c_s, c_r, e, ring * inner + to * pair + parity
+            ).start()
+
+        crecv[place] = cmid[place]
+
+    def gather_flat():
+        received(drecv.at[pl.ds(0, everyone - 1)], d_r)
+        dec_sum = jnp.sum(drecv[...].astype(F32), axis=0).astype(BF16)
+        agsend[...] = dec_sum
+        dall[parity, mine, piece_rows(ring)] = dec_sum
+        all_start(
+            lambda member, row, around: agsend,
+            dall.at[parity, mine, piece_rows(ring)],
+            a_s,
+            a_r,
+        )
+
+    def gather_planes():
+        received(drecv.at[pl.ds(0, half - 1)], d_r)
+        dec_plane = jnp.sum(drecv[...].astype(F32), axis=0).astype(BF16)
+        zsend[...] = dec_plane
+        zrecv[ring] = dec_plane
+
+        @pl.loop(1, outer)
+        def _(i):
+            to = lax.rem(ring + i, outer)
+            remote(zsend, zrecv.at[ring], z_s, z_r, e, to * inner + seat).start()
+
+        if rows_in > 1:
+            received(crecv.at[pl.ds(0, rows_in - 1)], c_r)
+        wo_plane = jnp.sum(crecv[...].astype(F32), axis=0).astype(BF16)
+        for o in range(outer):
+            fsend[o] = wo_plane[o * wo_rows : (o + 1) * wo_rows]
+        spot = e * outer + ring
+        frecv[spot] = fsend[ring]
+
+        @pl.loop(1, spots)
+        def _(i):
+            to = lax.rem(spot + i, spots)
+            ens, around = lax.div(to, outer), lax.rem(to, outer)
+            remote(fsend.at[around], frecv.at[spot], f_s, f_r, ens, around * inner + seat).start()
+
+        if outer > 1:
+            received(zrecv.at[pl.ds(0, outer - 1)], z_r)
+        dec_sum = jnp.sum(zrecv[...].astype(F32), axis=0).astype(BF16)
+        agsend[...] = dec_sum
+        dall[parity, mine] = dec_sum
+        plane_start(agsend, dall.at[parity, mine], a_s, a_r)
+
+    stats = slab[...]
     for p in range(pairs):
         columns = columns_of(p)
-        grads = split_heads(go[:, columns])
         attn_prob = prob[p]
-        grad_prob = dot(grads, extended(1, v_ref, columns), NT)
+        grad_prob = dot(split_heads(go[:, columns]), extended(1, v_ref, columns), NT)
         row_delta = jnp.sum(attn_prob * grad_prob, axis=-1, keepdims=True)
-        grad_scores = (attn_prob * (grad_prob - row_delta)).astype(BF16)
-        value_term = dot(attn_prob.astype(BF16), grads, TN)
-        key_term = dot(grad_scores, qs[p], TN)
-        for item, term, mid in ((0, key_term, kmid), (1, value_term, vmid)):
-            bsend[0, p, item] = term[0:nodes].astype(BF16)
-            bsend[1, p, item] = term[2 * nodes :].astype(BF16)
-            mid[:, columns] = term[nodes : 2 * nodes]
-        for slot, shift, present in sides:
-            out = remote(
-                bsend.at[slot, p],
-                brecv.at[1 - slot, p],
-                b_s.at[slot],
-                b_r.at[1 - slot],
-                e,
-                s + shift,
-            )
-            under(present, out.start)
-        gq_ref[:, columns] = (
-            merge_heads(dot(grad_scores, extended(0, k_ref, columns))) * scale
-        ).astype(BF16)
-
-    gs_ref[...] = dot(q_rows, decp[...]).astype(BF16)
-    received(drecv.at[pl.ds(0, group - 1)], d_r)
-    dec_plane = jnp.sum(drecv[...].astype(F32), axis=0).astype(BF16)
-    zsend[...] = dec_plane
-    zrecv[ring] = dec_plane
-    if outer > 3:
-        hello_wait()
-    for _ in range(outer - 4):
-        hello()
-        hello_wait()
-    outer_start(0)
-
-    received(crecv.at[pl.ds(0, group - 1)], c_r)
-    wo_plane = jnp.sum(crecv[...].astype(F32), axis=0).astype(BF16)
-    for o in range(outer):
-        fsend[o] = wo_plane[o * wo_rows : (o + 1) * wo_rows]
-    frecv[ring] = fsend[ring]
-    outer_start(1)
-
-    if outer > 1:
-        received(zrecv.at[pl.ds(0, outer - 1)], z_r)
-    dec_sum = jnp.sum(zrecv[...].astype(F32), axis=0).astype(BF16)
-    agsend[...] = dec_sum
-    dall[mine] = dec_sum
-    plane_start(2)
-
-    for slot, _, present in sides:
-        under(present, functools.partial(received, brecv.at[slot], b_r.at[slot]))
+        gsc[p] = (attn_prob * (grad_prob - row_delta)).astype(BF16)
+        stats = put_stat(stats, 2 * pairs + p, row_delta)
+    stat[...] = stats.T[0 : stat.shape[0]]
+    wo_across()
+    to_sides(stat, stat_near, st_s, st_r)
+    to_sides(q_ref, qn, qn_s, qn_r)
+    if flat:
+        gather_flat()
     for p in range(pairs):
         columns = columns_of(p)
-        for item, mid, out_ref in ((0, kmid, gk_ref), (1, vmid, gv_ref)):
-            out_ref[:, columns] = (
-                mid[:, columns]
-                + brecv[0, p, item].astype(F32)
-                + brecv[1, p, item].astype(F32)
-            ).astype(BF16)
-
-    if outer > 1:
-        received(frecv.at[pl.ds(0, outer - 1)], f_r)
+        middle = slice(nodes, 2 * nodes)
+        grads = split_heads(go[:, columns])
+        kmid[:, columns] = dot(gsc[p, :, middle], qs[p], TN)
+        vmid[:, columns] = dot(prob[p, :, middle].astype(BF16), grads, TN)
+        gq_ref[:, columns] = (
+            merge_heads(dot(gsc[p], extended(0, k_ref, columns))) * scale
+        ).astype(BF16)
+
+    gs_ref[...] = dot(q_rows, decp[...]).astype(BF16)
+    if not flat:
+        gather_planes()
+    for slot, _, present in sides:
+        under(present, functools.partial(received, rows_near.at[slot], n_r_sem.at[slot]))
+        under(present, functools.partial(received, qn.at[slot], qn_r.at[slot]))
+        under(present, functools.partial(received, stat_near.at[slot], st_r.at[slot]))
+    for slot in range(2):
+        go_near[slot] = dot(rows_near[slot], mix[...]).astype(BF16)
+    key_column = (
+        s * nodes + lax.broadcasted_iota(jnp.int32, (nodes, 2 * heads_rows), 0)
+    ).astype(F32)
+
+    def near_stat(at):
+        return jnp.concatenate([stat_near[i, at : at + 1, :] for i in range(2)], axis=1)
+
+    allowed = (key_column >= near_stat(3 * pairs)) & (key_column < near_stat(3 * pairs + 1))
+    for p in range(pairs):
+        columns = columns_of(p)
+        q_near = jnp.concatenate(
+            [split_heads(qn[i, :, columns].astype(F32) * scale) for i in range(2)], axis=0
+        )
+        g_near = jnp.concatenate([split_heads(go_near[i, :, columns]) for i in range(2)], axis=0)
+        scores = dot(k_ref[:, columns], q_near, NT)
+        near_prob = jnp.exp(
+            jnp.where(allowed, scores - near_stat(p), MASKED_SCORE)
+        ) * near_stat(pairs + p)
+        near_grad = dot(v_ref[:, columns], g_near, NT)
+        near_scores = near_prob * (near_grad - near_stat(2 * pairs + p))
+        gv_ref[:, columns] = (
+            vmid[:, columns] + dot(near_prob.astype(BF16), g_near)
+        ).astype(BF16)
+        gk_ref[:, columns] = (
+            kmid[:, columns] + dot(near_scores.astype(BF16), q_near)
+        ).astype(BF16)
+
+    if frecv.shape[0] > 1:
+        received(frecv.at[pl.ds(0, frecv.shape[0] - 1)], f_r)
     wo_sum = jnp.sum(frecv[...].astype(F32), axis=0)
     gwo_ref[...] = dot(wo_sum.astype(BF16), decp[...])
 
@@ -482,22 +662,37 @@
         def drain():
             for _ in range(n_e):
                 sent(text.at[1, 0], t_s.at[1 + shift])
-            sent(kh.at[slot], kv_s.at[slot])
+            for item in range(2):
+                sent(kh.at[slot, item], kv_s.at[slot, item])
             sent(qsend.at[slot], q_s.at[slot])
-            sent(bsend.at[slot], b_s.at[slot])
+            sent(qn.at[slot], qn_s.at[slot])
+            sent(rows_own, n_s_sem.at[slot])
+            sent(stat, st_s.at[slot])
 
         under(present, drain)
     if n_e > 1:
         sent(text.at[1, pl.ds(0, n_e - 1)], t_s.at[1])
-    sent(dsend.at[pl.ds(0, group - 1)], d_s)
-    sent(crecv.at[pl.ds(0, group - 1)], c_s)
-    if outer > 1:
-        sent(zrecv.at[pl.ds(0, outer - 1)], z_s)
-        sent(frecv.at[pl.ds(0, outer - 1)], f_s)
-    received(dall.at[pl.ds(0, group - 1)], a_r)
+    if pair > 1:
+        sent(dpair, pd_s)
+        sent(cpair, pc_s)
+    parts = drecv.shape[0]
+    sent(drecv.at[pl.ds(0, parts - 1)], d_s)
+    if not flat:
+        if rows_in > 1:
+            sent(crecv.at[pl.ds(0, rows_in - 1)], c_s)
+        if outer > 1:
+            sent(zrecv.at[pl.ds(0, outer - 1)], z_s)
+    if frecv.shape[0] > 1:
+        sent(frecv.at[pl.ds(0, frecv.shape[0] - 1)], f_s)
+    received(drecv.at[pl.ds(0, parts - 1)], a_r)
+    pair_start(dall.at[parity], dall.at[parity], pa_s, pa_r)
+    sent(drecv.at[pl.ds(0, parts - 1)], a_s)
+    if pair > 1:
+        received(dpair, pa_r)
     for c in range(group):
-        gdec_ref[:, c * lanes : (c + 1) * lanes] = dall[c].astype(F32)[0:n_var]
-    sent(dall.at[pl.ds(0, group - 1)], a_s)
+        gdec_ref[:, c * lanes : (c + 1) * lanes] = dall[c // half, c % half].astype(F32)[0:n_var]
+    if pair > 1:
+        sent(dpair, pa_s)
 
 
 def hand_over(*refs):
@@ -529,16 +724,21 @@
     n_e, n_s = lax.axis_size("ens"), lax.axis_size("space")
     inner = math.gcd(n_s, INNER)
     outer, group = n_s // inner, n_e * inner
+    pair = math.gcd(inner, 2)
+    half = group // pair
     nodes, width = node_states.shape[1:]
     att = query.shape[2]
     n_var, points = target.shape
     pairs = att // LANES
     var_pad = -(-n_var // LANES) * LANES
-    var_rows = -(-n_var // 16) * 16
+    flat = var_pad % (16 * outer) == 0
+    var_rows = var_pad if flat else -(-n_var // 16) * 16
+    piece = var_rows // outer if flat else var_rows
     lanes = width // group
     wo_rows = att // n_s
     span = 3 * nodes
     heads_per = LANES // HEAD_DIM
+    stat_rows = -(-(3 * pairs + 2) // 8) * 8
     dma = pltpu.SemaphoreType.DMA
     operands = (
         node_states[0],
@@ -582,26 +782,46 @@
             pltpu.VMEM((nodes, att), BF16),
             pltpu.VMEM((nodes, att), F32),
             pltpu.VMEM((nodes, att), F32),
-            pltpu.VMEM((2, pairs, 2, nodes, LANES), BF16),
-            pltpu.VMEM((2, pairs, 2, nodes, LANES), BF16),
-            pltpu.VMEM((inner, outer * wo_rows, var_pad), BF16),
-            pltpu.VMEM((group, outer * wo_rows, var_pad), BF16),
-            pltpu.VMEM((group, var_rows, lanes), BF16),
-            pltpu.VMEM((group, var_rows, lanes), BF16),
+            pltpu.VMEM((pairs, heads_per * nodes, span), BF16),
+            pltpu.VMEM((2, nodes, att), BF16),
+            pltpu.VMEM((nodes, var_pad), BF16),
+            pltpu.VMEM((2, nodes, var_pad), BF16),
+            pltpu.VMEM((heads_per * nodes, LANES), F32),
+            pltpu.VMEM((stat_rows, heads_per * nodes), F32),
+            pltpu.VMEM((2, stat_rows, heads_per * nodes), F32),
+            pltpu.VMEM((2, nodes, att), BF16),
+            pltpu.VMEM((pair, inner // pair, outer * wo_rows, var_pad), BF16),
+            pltpu.VMEM((inner // pair, outer * wo_rows, var_pad), BF16),
+            pltpu.VMEM((inner // pair, outer * wo_rows, var_pad), BF16),
+            pltpu.VMEM((inner // pair, outer * wo_rows, var_pad), BF16),
+            pltpu.VMEM((pair, half, var_rows, lanes), BF16),
+            pltpu.VMEM((half, var_rows, lanes), BF16),
+            pltpu.VMEM((half, var_rows, lanes), BF16),
+            pltpu.VMEM((half * outer if flat else half, piece, lanes), BF16),
             pltpu.VMEM((var_rows, lanes), BF16),
             pltpu.VMEM((outer, var_rows, lanes), BF16),
             pltpu.VMEM((outer, wo_rows, var_pad), BF16),
-            pltpu.VMEM((outer, wo_rows, var_pad), BF16),
-            pltpu.VMEM((var_rows, lanes), BF16),
-            pltpu.VMEM((group, var_rows, lanes), BF16),
-            dma((2,)),
-            dma((2,)),
+            pltpu.VMEM(((half if flat else n_e) * outer, wo_rows, var_pad), BF16),
+            pltpu.VMEM((piece, lanes), BF16),
+            pltpu.VMEM((pair, half, var_rows, lanes), BF16),
+            dma((2, 2)),
+            dma((2, 2)),
             dma((3,)),
             dma((3,)),
             dma((2,)),
             dma((2,)),
             dma((2,)),
             dma((2,)),
+            dma((2,)),
+            dma((2,)),
+            dma((2,)),
+            dma((2,)),
+            dma,
+            dma,
+            dma,
+            dma,
+            dma,
+            dma,
             dma,
             dma,
             dma,

time: 32.6 us -> 30.2 us (0.926)
  Pallas kernels: 31.4 us -> 29.3 us
    pallas_call x1, Pallas kernels: 30.3 us -> 28.3 us  [per_device(): pl.pallas_call(functools.partial(kernel, n_e, n_s), out_shape=(pltpu.VMEM...]
where the time goes in v2:
time: 30.2 us; the launch traced here: 30 us
  Pallas kernels  29.3 us (97%)
  between operations  0.64 us (2%)
    pallas_call x1, Pallas kernels, per_device(): pl.pallas_call(functools.partial(kernel, n_e, n_s), out_shape=(pltpu.VMEM...  28.3 us
    pallas_call x1, Pallas kernels, per_device(): pl.pallas_call(hand_over, out_shape=[jax.ShapeDtypeStruct(x.shape, x.dtyp...  1.07 us

profile of v2, /device:TPU:1, one launch (start us, length us, event | category | flops | bytes accessed | tf_op | source)
XLA Modules:
  0.0 30.0 jit_solution(1154468220854597844)
XLA Ops:
  0.6 28.3 %shard_map.163 = (bf16[128,1024]{1,0:T(8,128)(2,1)S(1)}, bf16[128,512]{1,0:T(8,128)(2,1)S(1)}, bf16[128,512]{1,0:T(8,128)(2,1)S(1)}, bf16[128,512]{1,0:T(8,128)(...) custom-call(bf16[128,1024]{1,0:T(8,128)(2,1)} %bitcast.11, bf16[128,512]{1,0:T(8,128)(2,1)} %bitcast.12, ...), custom_call_target="tpu_custom_call" | custom-call | tf_op jit(solution)/shard_map/pallas_call | solution.py:757
  28.9 1.1 %shard_map.164 = (bf16[128,1024]{1,0:T(8,128)(2,1)}, bf16[128,512]{1,0:T(8,128)(2,1)}, bf16[128,512]{1,0:T(8,128)(2,1)}, bf16[128,512]{1,0:T(8,128)(2,1)}, f32[32,1024]{1,0:T(8,128)}, /*index=5*/f32[100,1024]{1,0:T(8,128)}) custom-call(bf16[128,1024]{1,0:T(8,128)(2,1)S(1)} %get-tuple-element.18.refs_0_, bf16[128,512]{1,0:T(8,128)(2,1)S(1)} %get-tuple-element.19.refs_1_, ...), custom_call_target="tpu_custom_call" | custom-call | tf_op jit(solution)/shard_map/pallas_call | solution.py:842

commit v3 on v2

--- a/solution.py
+++ b/solution.py
@@ -277,19 +277,24 @@
             s + shift,
         )
 
-    def to_sides(src, dst, s_sem, r_sem):
+    def to_sides(src, dst, s_sem, r_sem, when=(None, None)):
         for slot, shift, present in sides:
-            out = remote(
-                src, dst.at[1 - slot], s_sem.at[slot], r_sem.at[1 - slot], e, s + shift
-            )
-            under(present, out.start)
-
-    def start_kv(item):
+            if when[slot] is not False:
+                out = remote(
+                    src, dst.at[1 - slot], s_sem.at[slot], r_sem.at[1 - slot], e, s + shift
+                )
+                under(present if when[slot] is None else present & when[slot], out.start)
+
+    last_seat = seat == inner - 1
+
+    def start_kv(item, when=(None, None)):
         for slot, shift, present in sides:
-            under(present, kv_copy(slot, shift, item).start)
+            if when[slot] is not False:
+                shown = present if when[slot] is None else present & when[slot]
+                under(shown, kv_copy(slot, shift, item).start)
 
     loaded("k", "v")
-    start_kv(0)
+    start_kv(0, (None, jnp.logical_not(last_seat)))
 
     loaded("edges", "ew")
     first = (s - 1) * nodes
@@ -310,6 +315,7 @@
         received(text.at[1, pl.ds(0, n_e - 1)], t_r.at[1])
     for slot, _, present in sides:
         under(present, functools.partial(received, text.at[2 * slot], t_r.at[2 * slot]))
+    start_kv(0, (False, last_seat))
     if outer > 1:
         hello_wait()
         hello()
@@ -340,7 +346,7 @@
             qsend.at[slot], qrecv.at[1 - slot], q_s.at[slot], q_r.at[1 - slot], e, s + shift
         )
         under(present, out.start)
-    start_kv(1)
+    start_kv(1, (None, jnp.logical_not(last_seat)))
 
     blocks = win_ref.shape[0]
     key_place = first + lax.broadcasted_iota(jnp.int32, (1, 3 * nodes), 1)
@@ -378,10 +384,89 @@
         for slot, _, present in sides:
             under(present, functools.partial(received, kh.at[slot, item], kv_r.at[slot, item]))
 
-    arrived(0)
     if outer > 2:
         hello_wait()
         hello()
+    for slot, _, present in sides:
+        under(present, functools.partial(received, qrecv.at[slot], q_r.at[slot]))
+    start_kv(1, (False, last_seat))
+    to_sides(q_ref, qn, qn_s, qn_r, (False, last_seat))
+    q_own = q_ext[:, nodes : 2 * nodes] + qrecv[0].astype(F32) + qrecv[1].astype(F32)
+    q_rows = q_own.T.astype(BF16)
+    rows_own[...] = q_rows
+    dec_term = dot(q_own.astype(BF16), states_ref[...])
+    var_rows, lanes = dsend.shape[2:]
+    for c in range(group):
+        dsend[c // half, c % half] = dec_term[0:var_rows, c * lanes : (c + 1) * lanes].astype(BF16)
+
+    def pair_start(source, target, s_sem, r_sem):
+        if pair > 1:
+            remote(source, target, s_sem, r_sem, e, s + 1 - 2 * parity).start()
+
+    def plane_start(source, target, s_sem, r_sem):
+        @pl.loop(1, half)
+        def _(i):
+            to = lax.rem(mine + i, half)
+            ens, row = lax.div(to, rows_in), lax.rem(to, rows_in)
+            remote(
+                source if source is agsend else source.at[to],
+                target,
+                s_sem,
+                r_sem,
+                ens,
+                ring * inner + row * pair + parity,
+            ).start()
+
+    pair_start(dsend.at[1 - parity], dpair, pd_s, pd_r)
+    to_sides(rows_own, rows_near, n_s_sem, n_r_sem)
+    go[...] = dot(q_rows, mix[...]).astype(BF16)
+    if outer > 3:
+        hello_wait()
+        hello()
+    if pair > 1:
+        received(dpair, pd_r)
+        dmid[...] = (dsend[parity].astype(F32) + dpair[...].astype(F32)).astype(BF16)
+    else:
+        dmid[...] = dsend[parity]
+    if outer > 1:
+        hello_wait()
+    for _ in range(outer - 4):
+        hello()
+        hello_wait()
+    if flat:
+        piece = drecv.shape[1]
+
+        def all_start(source_of, target, s_sem, r_sem):
+            for far in range(outer):
+                around = lax.rem(ring + far, outer)
+                for across in range(n_e):
+                    ens = lax.rem(e + across, n_e)
+                    for along in range(rows_in):
+                        if far or across or along:
+                            row = lax.rem(place + along, rows_in)
+                            remote(
+                                source_of(ens * rows_in + row, row, around),
+                                target,
+                                s_sem,
+                                r_sem,
+                                ens,
+                                around * inner + row * pair + parity,
+                            ).start()
+
+        def piece_rows(around):
+            return pl.ds(pl.multiple_of(around * piece, piece), piece)
+
+        all_start(
+            lambda member, row, around: dmid.at[member, piece_rows(around)],
+            drecv.at[seat_all],
+            d_s,
+            d_r,
+        )
+        drecv[seat_all] = dmid[mine, piece_rows(ring)]
+    else:
+        plane_start(dmid, drecv.at[mine], d_s, d_r)
+        drecv[mine] = dmid[mine]
+    arrived(0)
     heads_rows = heads_per * nodes
     stat_lane = lax.broadcasted_iota(jnp.int32, (heads_rows, LANES), 1)
 
@@ -426,83 +511,6 @@
         stats = put_stat(stats, pairs + p, inverse)
 
     slab[...] = stats
-    if outer > 3:
-        hello_wait()
-        hello()
-    for slot, _, present in sides:
-        under(present, functools.partial(received, qrecv.at[slot], q_r.at[slot]))
-    q_own = q_ext[:, nodes : 2 * nodes] + qrecv[0].astype(F32) + qrecv[1].astype(F32)
-    q_rows = q_own.T.astype(BF16)
-    rows_own[...] = q_rows
-    dec_term = dot(q_own.astype(BF16), states_ref[...])
-    var_rows, lanes = dsend.shape[2:]
-    for c in range(group):
-        dsend[c // half, c % half] = dec_term[0:var_rows, c * lanes : (c + 1) * lanes].astype(BF16)
-
-    def pair_start(source, target, s_sem, r_sem):
-        if pair > 1:
-            remote(source, target, s_sem, r_sem, e, s + 1 - 2 * parity).start()
-
-    def plane_start(source, target, s_sem, r_sem):
-        @pl.loop(1, half)
-        def _(i):
-            to = lax.rem(mine + i, half)
-            ens, row = lax.div(to, rows_in), lax.rem(to, rows_in)
-            remote(
-                source if source is agsend else source.at[to],
-                target,
-                s_sem,
-                r_sem,
-                ens,
-                ring * inner + row * pair + parity,
-            ).start()
-
-    pair_start(dsend.at[1 - parity], dpair, pd_s, pd_r)
-    to_sides(rows_own, rows_near, n_s_sem, n_r_sem)
-    go[...] = dot(q_rows, mix[...]).astype(BF16)
-    if pair > 1:
-        received(dpair, pd_r)
-        dmid[...] = (dsend[parity].astype(F32) + dpair[...].astype(F32)).astype(BF16)
-    else:
-        dmid[...] = dsend[parity]
-    if outer > 1:
-        hello_wait()
-    for _ in range(outer - 4):
-        hello()
-        hello_wait()
-    if flat:
-        piece = drecv.shape[1]
-
-        def all_start(source_of, target, s_sem, r_sem):
-            for far in range(outer):
-                around = lax.rem(ring + far, outer)
-                for across in range(n_e):
-                    ens = lax.rem(e + across, n_e)
-                    for along in range(rows_in):
-                        if far or across or along:
-                            row = lax.rem(place + along, rows_in)
-                            remote(
-                                source_of(ens * rows_in + row, row, around),
-                                target,
-                                s_sem,
-                                r_sem,
-                                ens,
-                                around * inner + row * pair + parity,
-                            ).start()
-
-        def piece_rows(around):
-            return pl.ds(pl.multiple_of(around * piece, piece), piece)
-
-        all_start(
-            lambda member, row, around: dmid.at[member, piece_rows(around)],
-            drecv.at[seat_all],
-            d_s,
-            d_r,
-        )
-        drecv[seat_all] = dmid[mine, piece_rows(ring)]
-    else:
-        plane_start(dmid, drecv.at[mine], d_s, d_r)
-        drecv[mine] = dmid[mine]
     arrived(1)
     for p in range(pairs):
         columns = columns_of(p)
@@ -525,20 +533,6 @@
         else:
             cmid[...] = csend[parity]
 
-        if flat:
-
-            def wo_part(around):
-                return pl.ds(pl.multiple_of(around * wo_rows, wo_rows), wo_rows)
-
-            all_start(
-                lambda member, row, around: cmid.at[row, wo_part(around)],
-                frecv.at[seat_all],
-                f_s,
-                f_r,
-            )
-            frecv[seat_all] = cmid[place, wo_part(ring)]
-            return
-
         @pl.loop(1, rows_in)
         def _(i):
             to = lax.rem(place + i, rows_in)
@@ -560,17 +554,7 @@
             a_r,
         )
 
-    def gather_planes():
-        received(drecv.at[pl.ds(0, half - 1)], d_r)
-        dec_plane = jnp.sum(drecv[...].astype(F32), axis=0).astype(BF16)
-        zsend[...] = dec_plane
-        zrecv[ring] = dec_plane
-
-        @pl.loop(1, outer)
-        def _(i):
-            to = lax.rem(ring + i, outer)
-            remote(zsend, zrecv.at[ring], z_s, z_r, e, to * inner + seat).start()
-
+    def wo_around():
         if rows_in > 1:
             received(crecv.at[pl.ds(0, rows_in - 1)], c_r)
         wo_plane = jnp.sum(crecv[...].astype(F32), axis=0).astype(BF16)
@@ -585,6 +569,18 @@
             ens, around = lax.div(to, outer), lax.rem(to, outer)
             remote(fsend.at[around], frecv.at[spot], f_s, f_r, ens, around * inner + seat).start()
 
+    def gather_planes():
+        received(drecv.at[pl.ds(0, half - 1)], d_r)
+        dec_plane = jnp.sum(drecv[...].astype(F32), axis=0).astype(BF16)
+        zsend[...] = dec_plane
+        zrecv[ring] = dec_plane
+
+        @pl.loop(1, outer)
+        def _(i):
+            to = lax.rem(ring + i, outer)
+            remote(zsend, zrecv.at[ring], z_s, z_r, e, to * inner + seat).start()
+
+        wo_around()
         if outer > 1:
             received(zrecv.at[pl.ds(0, outer - 1)], z_r)
         dec_sum = jnp.sum(zrecv[...].astype(F32), axis=0).astype(BF16)
@@ -603,9 +599,7 @@
     stat[...] = stats.T[0 : stat.shape[0]]
     wo_across()
     to_sides(stat, stat_near, st_s, st_r)
-    to_sides(q_ref, qn, qn_s, qn_r)
-    if flat:
-        gather_flat()
+    to_sides(q_ref, qn, qn_s, qn_r, (None, jnp.logical_not(last_seat)))
     for p in range(pairs):
         columns = columns_of(p)
         middle = slice(nodes, 2 * nodes)
@@ -617,7 +611,10 @@
         ).astype(BF16)
 
     gs_ref[...] = dot(q_rows, decp[...]).astype(BF16)
-    if not flat:
+    if flat:
+        gather_flat()
+        wo_around()
+    else:
         gather_planes()
     for slot, _, present in sides:
         under(present, functools.partial(received, rows_near.at[slot], n_r_sem.at[slot]))
@@ -652,6 +649,9 @@
             kmid[:, columns] + dot(near_scores.astype(BF16), q_near)
         ).astype(BF16)
 
+    parts = drecv.shape[0]
+    received(drecv.at[pl.ds(0, parts - 1)], a_r)
+    pair_start(dall.at[parity], dall.at[parity], pa_s, pa_r)
     if frecv.shape[0] > 1:
         received(frecv.at[pl.ds(0, frecv.shape[0] - 1)], f_r)
     wo_sum = jnp.sum(frecv[...].astype(F32), axis=0)
@@ -675,17 +675,13 @@
     if pair > 1:
         sent(dpair, pd_s)
         sent(cpair, pc_s)
-    parts = drecv.shape[0]
     sent(drecv.at[pl.ds(0, parts - 1)], d_s)
-    if not flat:
-        if rows_in > 1:
-            sent(crecv.at[pl.ds(0, rows_in - 1)], c_s)
-        if outer > 1:
-            sent(zrecv.at[pl.ds(0, outer - 1)], z_s)
+    if rows_in > 1:
+        sent(crecv.at[pl.ds(0, rows_in - 1)], c_s)
+    if not flat and outer > 1:
+        sent(zrecv.at[pl.ds(0, outer - 1)], z_s)
     if frecv.shape[0] > 1:
         sent(frecv.at[pl.ds(0, frecv.shape[0] - 1)], f_s)
-    received(drecv.at[pl.ds(0, parts - 1)], a_r)
-    pair_start(dall.at[parity], dall.at[parity], pa_s, pa_r)
     sent(drecv.at[pl.ds(0, parts - 1)], a_s)
     if pair > 1:
         received(dpair, pa_r)
@@ -801,7 +797,7 @@
             pltpu.VMEM((var_rows, lanes), BF16),
             pltpu.VMEM((outer, var_rows, lanes), BF16),
             pltpu.VMEM((outer, wo_rows, var_pad), BF16),
-            pltpu.VMEM(((half if flat else n_e) * outer, wo_rows, var_pad), BF16),
+            pltpu.VMEM((n_e * outer, wo_rows, var_pad), BF16),
             pltpu.VMEM((piece, lanes), BF16),
             pltpu.VMEM((pair, half, var_rows, lanes), BF16),
             dma((2, 2)),

time: 30.2 us -> 28.9 us (0.957)
  Pallas kernels: 29.3 us -> 28.1 us
    pallas_call x1, Pallas kernels: 28.3 us -> 27 us  [per_device(): pl.pallas_call(functools.partial(kernel, n_e, n_s), out_shape=(pltpu.VMEM...]
where the time goes in v3:
time: 28.9 us; the launch traced here: 28.7 us
  Pallas kernels  28.1 us (97%)
  between operations  0.64 us (2%)
    pallas_call x1, Pallas kernels, per_device(): pl.pallas_call(functools.partial(kernel, n_e, n_s), out_shape=(pltpu.VMEM...  27 us
    pallas_call x1, Pallas kernels, per_device(): pl.pallas_call(hand_over, out_shape=[jax.ShapeDtypeStruct(x.shape, x.dtyp...  1.07 us

profile of v3, /device:TPU:1, one launch (start us, length us, event | category | flops | bytes accessed | tf_op | source)
XLA Modules:
  0.0 28.7 jit_solution(15973609262692596054)
XLA Ops:
  0.6 27.0 %shard_map.163 = (bf16[128,1024]{1,0:T(8,128)(2,1)S(1)}, bf16[128,512]{1,0:T(8,128)(2,1)S(1)}, bf16[128,512]{1,0:T(8,128)(2,1)S(1)}, bf16[128,512]{1,0:T(8,128)(...) custom-call(bf16[128,1024]{1,0:T(8,128)(2,1)} %bitcast.11, bf16[128,512]{1,0:T(8,128)(2,1)} %bitcast.12, ...), custom_call_target="tpu_custom_call" | custom-call | tf_op jit(solution)/shard_map/pallas_call | solution.py:753
  27.7 1.1 %shard_map.164 = (bf16[128,1024]{1,0:T(8,128)(2,1)}, bf16[128,512]{1,0:T(8,128)(2,1)}, bf16[128,512]{1,0:T(8,128)(2,1)}, bf16[128,512]{1,0:T(8,128)(2,1)}, f32[32,1024]{1,0:T(8,128)}, /*index=5*/f32[100,1024]{1,0:T(8,128)}) custom-call(bf16[128,1024]{1,0:T(8,128)(2,1)S(1)} %get-tuple-element.18.refs_0_, bf16[128,512]{1,0:T(8,128)(2,1)S(1)} %get-tuple-element.19.refs_1_, ...), custom_call_target="tpu_custom_call" | custom-call | tf_op jit(solution)/shard_map/pallas_call | solution.py:838
